TPU v7x, 256 devices: a whole 4x4x8 slice. The times are simulated.
256 devices in a mesh: dp: 32 (over z, y_hi, core), expert: 8 (over x, y_lo).
Axes of the slice: x: 4, y: 4 (y_hi: 2, y_lo: 2; y = y_hi * 2 + y_lo), z: 8, core: 2. Of those that a mesh axis runs over, the one named last changes fastest.
Arguments:
- tokens: bfloat16 [32768, 2048], P(('dp', 'expert')), may hold values from -24 to 24
- cotangent: bfloat16 [32768, 2048], P(('dp', 'expert')), may hold values from -24 to 24
- expert_ids: int32 [32768, 2], P(('dp', 'expert')), may hold values from 0 to 7, all different within a row; in each aligned block of 128 rows (0 to 127, 128 to 255, ...) at most 40 rows name the same one
- gate_weights: float32 [32768, 2], P(('dp', 'expert')), may hold values from 0.1 to 1
- partner: int32 [8], replicated, may hold values from 0 to 7, as said below
- w_gate: bfloat16 [8, 2048, 768], P('expert'), may hold values from -0.125 to 0.125
- w_up: bfloat16 [8, 2048, 768], P('expert'), may hold values from -0.125 to 0.125
- w_down: bfloat16 [8, 768, 2048], P('expert'), may hold values from -0.21875 to 0.21875
Outputs:
- mixed_out: bfloat16 [32768, 2048], P(('dp', 'expert'))
- token_grad: bfloat16 [32768, 2048], P(('dp', 'expert'))
- gate_grad: float32 [32768, 2], P(('dp', 'expert'))
- slot_grad_gate: float32 [8, 2048, 768], P('expert', 'dp')
- slot_grad_up: float32 [8, 2048, 768], P('expert', 'dp')
- slot_grad_down: float32 [8, 768, 2048], P('expert', None, 'dp')
Inputs may be any that keep to these rules, and one draw needn't show every extreme that they name: `expert_ids`: each row names 2 different experts. Among the 128 rows of one device no expert is named by more than 40 rows, and in every draw some device names some expert exactly 40 times. partner[partner[i]] = i and partner[i] != i for every slot i.
All inputs are finite; a program needn't handle non-finite values.
Results may differ from a plain program's by a relative error of at most 0.015.
Values may be sent and summed in bfloat16 or wider, within the bound.
A program may use at most 128 MiB of HBM per device.

v0:
```python
import jax
import jax.numpy as jnp
from jax import lax
from jax.sharding import PartitionSpec as P


def as_sent(shard):

    def short(part):
        return part.astype(jnp.bfloat16) if part.dtype == jnp.float32 else part

    return jax.tree.map(short, shard)


def contract_rows(left_mat, right_mat):
    return lax.dot_general(
        left_mat, right_mat, (((0,), (0,)), ((), ())), preferred_element_type=jnp.float32
    )


def contract_cols(left_mat, right_mat):
    return lax.dot_general(
        left_mat, right_mat, (((1,), (1,)), ((), ())), preferred_element_type=jnp.float32
    )


def pick_from(stacked, source):
    return lax.dynamic_index_in_dim(stacked, source, 0, keepdims=False)


def shards(tokens, cotangent, expert_ids, gate_weights, partner, w_gate, w_up, w_down):
    groups = lax.axis_size("expert")
    my_group = lax.axis_index("expert")
    tok_count, model_width = tokens.shape
    top_count = expert_ids.shape[1]
    capacity = min(tok_count, 5 * tok_count * top_count // (4 * groups))
    buffer_rows = groups * capacity
    group_ids = jnp.arange(groups, dtype=jnp.int32)
    my_mate = pick_from(partner, my_group)
    flat_ids = expert_ids.reshape(-1)
    dest_group = jnp.sum(
        jnp.where(flat_ids[:, None] == group_ids[None, :], partner[None, :], 0), axis=1
    )
    one_hot = (dest_group[:, None] == group_ids[None, :]).astype(jnp.int32)
    earlier = jnp.cumsum(one_hot, axis=0) - one_hot
    slot_index = dest_group * capacity + jnp.sum(earlier * one_hot, axis=1)
    place_mat = (slot_index[None, :] == jnp.arange(buffer_rows, dtype=jnp.int32)[:, None]).astype(
        jnp.bfloat16
    )
    replicas = lax.axis_size("dp")
    share_rows = model_width // replicas
    share_start = lax.axis_index("dp") * share_rows
    shares = (
        lax.dynamic_slice_in_dim(w_gate[0], share_start, share_rows, 0),
        lax.dynamic_slice_in_dim(w_up[0], share_start, share_rows, 0),
        lax.dynamic_slice_in_dim(w_down[0], share_start, share_rows, 1),
    )
    is_mate = (partner == my_group)[:, None, None]
    outgoing = tuple(
        (
            jnp.where(is_mate, own_share[None], jnp.zeros_like(own_share)[None])
            for own_share in shares
        )
    )
    incoming = jax.tree.map(
        lambda part, own: part.astype(own.dtype),
        lax.all_to_all(as_sent(outgoing), "expert", split_axis=0, concat_axis=0, tiled=True),
        outgoing,
    )
    mate_shares = tuple((pick_from(block_piece, my_mate) for block_piece in incoming))
    gate_mat, up_mat, down_mat = (
        lax.all_gather(mate_shares[0], "dp", axis=0, tiled=True),
        lax.all_gather(mate_shares[1], "dp", axis=0, tiled=True),
        lax.all_gather(mate_shares[2], "dp", axis=1, tiled=True),
    )
    repeated = jnp.repeat(tokens, top_count, axis=0)
    outgoing_rows = jnp.dot(place_mat, repeated, preferred_element_type=jnp.float32).astype(
        jnp.bfloat16
    )
    expert_in = lax.all_to_all(
        outgoing_rows.reshape(groups, capacity, model_width),
        "expert",
        split_axis=0,
        concat_axis=0,
        tiled=True,
    ).reshape(buffer_rows, model_width)
    gate_pre = jnp.dot(expert_in, gate_mat, preferred_element_type=jnp.float32)
    up_pre = jnp.dot(expert_in, up_mat, preferred_element_type=jnp.float32)
    sigmoid_gate = jax.nn.sigmoid(gate_pre)
    hidden = (gate_pre * sigmoid_gate * up_pre).astype(jnp.bfloat16)
    expert_out = jnp.dot(hidden, down_mat, preferred_element_type=jnp.float32).astype(jnp.bfloat16)
    returned = lax.all_to_all(
        expert_out.reshape(groups, capacity, model_width),
        "expert",
        split_axis=0,
        concat_axis=0,
        tiled=True,
    ).reshape(buffer_rows, model_width)
    per_assign = (
        jnp.take(returned, slot_index, axis=0)
        .astype(jnp.float32)
        .reshape(tok_count, top_count, model_width)
    )
    mixed_out = jnp.sum(gate_weights[:, :, None] * per_assign, axis=1).astype(jnp.bfloat16)
    cot_float = cotangent.astype(jnp.float32)
    gate_grad = jnp.sum(cot_float[:, None, :] * per_assign, axis=2)
    scaled = (
        (gate_weights[:, :, None] * cot_float[:, None, :])
        .astype(jnp.bfloat16)
        .reshape(-1, model_width)
    )
    outgoing_grads = jnp.dot(place_mat, scaled, preferred_element_type=jnp.float32).astype(
        jnp.bfloat16
    )
    grads_in = lax.all_to_all(
        outgoing_grads.reshape(groups, capacity, model_width),
        "expert",
        split_axis=0,
        concat_axis=0,
        tiled=True,
    ).reshape(buffer_rows, model_width)
    hidden_grad = contract_cols(grads_in, down_mat)
    gate_grad_pre = (
        hidden_grad * up_pre * sigmoid_gate * (1.0 + gate_pre * (1.0 - sigmoid_gate))
    ).astype(jnp.bfloat16)
    up_grad_pre = (hidden_grad * gate_pre * sigmoid_gate).astype(jnp.bfloat16)
    row_grad = (contract_cols(gate_grad_pre, gate_mat) + contract_cols(up_grad_pre, up_mat)).astype(
        jnp.bfloat16
    )
    returned_grads = lax.all_to_all(
        row_grad.reshape(groups, capacity, model_width),
        "expert",
        split_axis=0,
        concat_axis=0,
        tiled=True,
    ).reshape(buffer_rows, model_width)
    grad_rows = (
        jnp.take(returned_grads, slot_index, axis=0)
        .astype(jnp.float32)
        .reshape(tok_count, top_count, model_width)
    )
    token_grad = jnp.sum(grad_rows, axis=1).astype(jnp.bfloat16)
    partial_gate = contract_rows(expert_in, gate_grad_pre)
    partial_up = contract_rows(expert_in, up_grad_pre)
    partial_down = contract_rows(hidden, grads_in)
    sum_gate, sum_up, sum_down = (
        lax.psum_scatter(
            partial_gate.astype(jnp.bfloat16), "dp", scatter_dimension=0, tiled=True
        ).astype(jnp.float32),
        lax.psum_scatter(
            partial_up.astype(jnp.bfloat16), "dp", scatter_dimension=0, tiled=True
        ).astype(jnp.float32),
        lax.psum_scatter(
            partial_down.astype(jnp.bfloat16), "dp", scatter_dimension=1, tiled=True
        ).astype(jnp.float32),
    )
    return (mixed_out, token_grad, gate_grad, sum_gate[None], sum_up[None], sum_down[None])


def solution(mesh):
    in_specs = (
        P(("dp", "expert"), None),
        P(("dp", "expert"), None),
        P(("dp", "expert"), None),
        P(("dp", "expert"), None),
        P(),
        P("expert", None, None),
        P("expert", None, None),
        P("expert", None, None),
    )
    out_specs = (
        P(("dp", "expert"), None),
        P(("dp", "expert"), None),
        P(("dp", "expert"), None),
        P("expert", "dp", None),
        P("expert", "dp", None),
        P("expert", None, "dp"),
    )
    return jax.shard_map(shards, mesh=mesh, in_specs=in_specs, out_specs=out_specs, check_vma=False)
```

profile of v0, /device:TPU:4, one launch (start us, length us, event | category | flops | bytes accessed | tf_op | source)
XLA Modules:
  0.0 688.2 jit_solution(8233593337685913203)
XLA Ops:
  10.5 6.3 all-to-all-start.2
  19.3 7.3 %all-to-all-done.2 = bf16[8,64,768]{2,1,0:T(8,128)(2,1)} async-done(((bf16[8,64,768]{2,1,0:T(8,128)(2,1)}), bf16[8,64,768]{2,1,0:T(8,128)(2,1)}, u32[]{:S(2)}, u32[]{:S(2)}) %all-to-all-start.2) | async-done | bytes 786464 | tf_op jit(solution)/shard_map/all_to_all | solution.py:67
  28.7 15.4 %all_to_all.35 = bf16[8,768,64]{1,2,0:T(8,128)(2,1)S(1)} all-to-all(bf16[8,768,64]{1,2,0:T(8,128)(2,1)S(1)} %broadcast_select_fusion.1), channel_id=1, replica_groups=mesh['dp'=32,'expert'=8] {'expert'}, dimensions={0} | all-to-all | bytes 1572864 | tf_op jit(solution)/shard_map/all_to_all | solution.py:67
  44.8 13.8 %all_to_all.36 = bf16[8,64,768]{2,1,0:T(8,128)(2,1)S(1)} all-to-all(bf16[8,64,768]{2,1,0:T(8,128)(2,1)S(1)} %copy-done.6), channel_id=1, replica_groups=mesh['dp'=32,'expert'=8] {'expert'}, dimensions={0} | all-to-all | bytes 1572864 | tf_op jit(solution)/shard_map/all_to_all | solution.py:67
  63.2 6.2 all-to-all-start
  69.5 2.4 mul.83
  71.9 2.7 mul.84
  76.5 6.3 all-to-all-done
  82.8 7.1 %all-to-all-start.5 = ((bf16[8,40,2048]{2,1,0:T(8,128)(2,1)}), bf16[8,40,2048]{2,1,0:T(8,128)(2,1)}, u32[]{:S(2)}, u32[]{:S(2)}) async-start(bf16[8,40,2048]{2,1,0:T(8,128)(2,1)} %bitcast.70), calls=%async_computation.5 | async-start | bytes 2621440 | tf_op jit(solution)/shard_map/all_to_all | solution.py:115
  89.9 34.6 %all-gather.9.cloned.1.call-done = bf16[1,2048,768]{2,1,0:T(8,128)(2,1)} async-done(((bf16[1,64,768]{2,1,0:T(8,128)(2,1)}), bf16[1,2048,768]{2,1,0:T(8,128)(2,1)}) %all-gather.9.cloned.1.call-update) | async-done | bytes 3145744 | tf_op jit(solution)/shard_map/all_gather | solution.py:73
  124.5 3.5 fusion.6
  128.0 79.0 %all-gather.11.cloned.1.call-done = bf16[1,768,2048]{1,2,0:T(8,128)(2,1)} async-done(((bf16[1,768,64]{1,2,0:T(8,128)(2,1)}), bf16[1,768,2048]{1,2,0:T(8,128)(2,1)}) %all-gather.11.cloned.1.call-update) | async-done | bytes 3145744 | tf_op jit(solution)/shard_map/all_gather | solution.py:74
  206.9 3.5 fusion
  210.4 79.6 %all-gather.7.cloned.1.call-done = bf16[1,2048,768]{2,1,0:T(8,128)(2,1)} async-done(((bf16[1,64,768]{2,1,0:T(8,128)(2,1)}), bf16[1,2048,768]{2,1,0:T(8,128)(2,1)}) %all-gather.7.cloned.1.call-update) | async-done | bytes 3145744 | tf_op jit(solution)/shard_map/all_gather | solution.py:72
  290.0 3.7 multiply_convert_fusion.3
  294.5 4.8 convolution_convert_fusion
  299.6 4.9 convolution_convert_fusion.1
  304.5 4.8 convolution_convert_fusion.2
  309.4 3.3 fusion.4
  315.1 5.0 all-to-all-start.6
  320.0 4.3 fusion.18
  324.3 12.7 %all-to-all-done.6 = bf16[8,40,2048]{2,1,0:T(8,128)(2,1)S(1)} async-done(((bf16[8,40,2048]{2,1,0:T(8,128)(2,1)}), bf16[8,40,2048]{2,1,0:T(8,128)(2,1)S(1)}, u32[]{:S(2)}, u32[]{:S(2)}) %all-to-all-start.6) | async-done | bytes 1310752 | tf_op jit(solution)/shard_map/all_to_all | solution.py:130
  337.0 7.2 %all-to-all-start.4 = ((bf16[8,40,2048]{2,1,0:T(8,128)(2,1)}), bf16[8,40,2048]{2,1,0:T(8,128)(2,1)S(1)}, u32[]{:S(2)}, u32[]{:S(2)}) async-start(bf16[8,40,2048]{2,1,0:T(8,128)(2,1)} %bitcast.71), calls=%async_computation.4 | async-start | bytes 2621440 | tf_op jit(solution)/shard_map/all_to_all | solution.py:92
  344.2 2.3 gather_fusion.1
  346.5 15.8 %all-to-all-done.4 = bf16[8,40,2048]{2,1,0:T(8,128)(2,1)S(1)} async-done(((bf16[8,40,2048]{2,1,0:T(8,128)(2,1)}), bf16[8,40,2048]{2,1,0:T(8,128)(2,1)S(1)}, u32[]{:S(2)}, u32[]{:S(2)}) %all-to-all-start.4) | async-done | bytes 1310752 | tf_op jit(solution)/shard_map/all_to_all | solution.py:92
  363.7 2.9 broadcast_select_fusion
  368.8 2.7 reshape.102
  372.7 4.7 reduce.1
  377.5 5.6 multiply_reduce_fusion.1
  383.1 45.0 %reduce-scatter.8.cloned.1.call-done = bf16[768,64]{0,1:T(8,128)(2,1)} async-done(((bf16[768,2048]{0,1:T(8,128)(2,1)}), bf16[768,64]{0,1:T(8,128)(2,1)}) %reduce-scatter.8.cloned.1.call-update) | async-done | bytes 98320 | tf_op jit(solution)/shard_map/reduce_scatter | solution.py:153
  429.7 124.2 %reduce-scatter.6.cloned.1.call-done = bf16[64,768]{1,0:T(8,128)(2,1)} async-done(((bf16[2048,768]{1,0:T(8,128)(2,1)}), bf16[64,768]{1,0:T(8,128)(2,1)}) %reduce-scatter.6.cloned.1.call-update) | async-done | bytes 98320 | tf_op jit(solution)/shard_map/reduce_scatter | solution.py:150
  555.5 124.2 %reduce-scatter.4.cloned.1.call-done = bf16[64,768]{1,0:T(8,128)(2,1)} async-done(((bf16[2048,768]{1,0:T(8,128)(2,1)}), bf16[64,768]{1,0:T(8,128)(2,1)}) %reduce-scatter.4.cloned.1.call-update) | async-done | bytes 98320 | tf_op jit(solution)/shard_map/reduce_scatter | solution.py:147
  (84 shorter events, 26.0 us)
Async XLA Ops:
  7.2 21.0 %copy-start = (bf16[1,768,2048]{2,1,0:T(8,128)(2,1)S(1)}, bf16[1,768,2048]{2,1,0:T(8,128)(2,1)}, u32[]{:S(2)}) copy-start(bf16[1,768,2048]{2,1,0:T(8,128)(2,1)} %param.17) | copy-start | bytes 9437188
  7.2 9.6 %copy-start.11 = (s32[8]{0:T(128)S(1)}, s32[8]{0:T(128)}, u32[]{:S(2)}) copy-start(s32[8]{0:T(128)} %param.14) | copy-start | bytes 100
  10.5 16.1 %all-to-all-start.2 = ((bf16[8,64,768]{2,1,0:T(8,128)(2,1)}), bf16[8,64,768]{2,1,0:T(8,128)(2,1)}, u32[]{:S(2)}, u32[]{:S(2)}) async-start(bf16[8,64,768]{2,1,0:T(8,128)(2,1)} %get-tuple-element.33), calls=%async_computation.2 | async-start | bytes 1572864 | tf_op jit(solution)/shard_map/all_to_all | solution.py:67
  16.8 107.7 %all-gather.9.cloned.1.call-start = ((), (), s32[]{:S(2)}) async-start(), calls=%async_computation.14 | async-start | bytes 3244032 | tf_op jit(solution)/shard_map/all_gather | solution.py:73
  28.2 178.8 %all-gather.11.cloned.1.call-start = ((), (), s32[]{:S(2)}) async-start(), calls=%async_computation.15 | async-start | bytes 3244032 | tf_op jit(solution)/shard_map/all_gather | solution.py:74
  28.4 16.4 %copy-start.6 = (bf16[8,64,768]{2,1,0:T(8,128)(2,1)S(1)}, bf16[8,64,768]{2,1,0:T(8,128)(2,1)}, u32[]{:S(2)}) copy-start(bf16[8,64,768]{2,1,0:T(8,128)(2,1)} %get-tuple-element.32) | copy-start | bytes 2359300
  28.5 30.8 %copy-start.9 = (s32[128,2]{0,1:T(2,128)S(1)}, s32[128,2]{0,1:T(2,128)}, u32[]{:S(2)}) copy-start(s32[128,2]{0,1:T(2,128)} %param.12) | copy-start | bytes 3076
  28.6 31.8 %copy-start.7 = (bf16[128,2048]{1,0:T(8,128)(2,1)S(1)}, bf16[128,2048]{1,0:T(8,128)(2,1)}, u32[]{:S(2)}) copy-start(bf16[128,2048]{1,0:T(8,128)(2,1)} %param.10) | copy-start | bytes 1572868
  44.7 245.3 %all-gather.7.cloned.1.call-start = ((), (), s32[]{:S(2)}) async-start(), calls=%async_computation.13 | async-start | bytes 3244032 | tf_op jit(solution)/shard_map/all_gather | solution.py:72
  61.7 7.8 %copy-start.8 = (bf16[128,2048]{1,0:T(8,128)(2,1)S(1)}, bf16[128,2048]{1,0:T(8,128)(2,1)}, u32[]{:S(2)}) copy-start(bf16[128,2048]{1,0:T(8,128)(2,1)} %param.11) | copy-start | bytes 1572868
  63.2 19.6 %all-to-all-start = ((bf16[8,40,2048]{2,1,0:T(8,128)(2,1)}), bf16[8,40,2048]{2,1,0:T(8,128)(2,1)}, u32[]{:S(2)}, u32[]{:S(2)}) async-start(bf16[8,40,2048]{2,1,0:T(8,128)(2,1)} %bitcast.3), calls=%async_computation | async-start | bytes 2621440 | tf_op jit(solution)/shard_map/all_to_all | solution.py:80
  71.9 2.7 copy-start.10
  74.6 8.2 %copy-start.2 = (f32[256,2048]{1,0:T(8,128)}, f32[256,2048]{1,0:T(8,128)S(1)}, u32[]{:S(2)}) copy-start(f32[256,2048]{1,0:T(8,128)S(1)} %mul.84) | copy-start | bytes 6291460
  82.8 45.1 %all-to-all-start.5 = ((bf16[8,40,2048]{2,1,0:T(8,128)(2,1)}), bf16[8,40,2048]{2,1,0:T(8,128)(2,1)}, u32[]{:S(2)}, u32[]{:S(2)}) async-start(bf16[8,40,2048]{2,1,0:T(8,128)(2,1)} %bitcast.70), calls=%async_computation.5 | async-start | bytes 2621440 | tf_op jit(solution)/shard_map/all_to_all | solution.py:115
  89.9 338.3 %reduce-scatter.8.cloned.1.call-start = ((), (), s32[]{:S(2)}) async-start(), calls=%async_computation.12 | async-start | bytes 3244032 | tf_op jit(solution)/shard_map/reduce_scatter | solution.py:153
  293.7 0.8 copy-start.15
  293.7 10.8 %copy-start.13 = (bf16[320,768]{1,0:T(8,128)(2,1)}, bf16[320,768]{1,0:T(8,128)(2,1)S(1)}, u32[]{:S(2)}) copy-start(bf16[320,768]{1,0:T(8,128)(2,1)S(1)} %get-tuple-element.27) | copy-start | bytes 1474564
  299.4 254.6 %reduce-scatter.6.cloned.1.call-start = ((), (), s32[]{:S(2)}) async-start(), calls=%async_computation.11 | async-start | bytes 3244032 | tf_op jit(solution)/shard_map/reduce_scatter | solution.py:150
  304.5 375.3 %reduce-scatter.4.cloned.1.call-start = ((), (), s32[]{:S(2)}) async-start(), calls=%async_computation.10 | async-start | bytes 3244032 | tf_op jit(solution)/shard_map/reduce_scatter | solution.py:147
  309.4 3.3 copy-start.12
  309.4 3.3 copy-start.14
  315.1 5.0 copy-start.16
  315.1 21.9 %all-to-all-start.6 = ((bf16[8,40,2048]{2,1,0:T(8,128)(2,1)}), bf16[8,40,2048]{2,1,0:T(8,128)(2,1)S(1)}, u32[]{:S(2)}, u32[]{:S(2)}) async-start(bf16[8,40,2048]{2,1,0:T(8,128)(2,1)} %bitcast.16), calls=%async_computation.6 | async-start | bytes 2621440 | tf_op jit(solution)/shard_map/all_to_all | solution.py:130
  337.0 25.4 %all-to-all-start.4 = ((bf16[8,40,2048]{2,1,0:T(8,128)(2,1)}), bf16[8,40,2048]{2,1,0:T(8,128)(2,1)S(1)}, u32[]{:S(2)}, u32[]{:S(2)}) async-start(bf16[8,40,2048]{2,1,0:T(8,128)(2,1)} %bitcast.71), calls=%async_computation.4 | async-start | bytes 2621440 | tf_op jit(solution)/shard_map/all_to_all | solution.py:92
  363.7 2.9 copy-start.4
  366.6 4.9 copy-start.5
  368.8 2.7 copy-start.3
  372.7 308.6 %copy-start.1 = (bf16[1,768,2048]{2,1,0:T(8,128)(2,1)S(1)}, bf16[1,768,2048]{2,1,0:T(8,128)(2,1)}, u32[]{:S(2)}) copy-start(bf16[1,768,2048]{2,1,0:T(8,128)(2,1)} %param.17) | copy-start | bytes 9437188
Sparse Core Ops, SparseCore 0:
  28.3 96.1 all-gather.8
  127.8 79.0 all-gather.10
  210.3 79.6 all-gather.6
  299.5 128.6 reduce-scatter.7
  432.2 121.7 reduce-scatter.5
  558.0 121.7 reduce-scatter.3
where the time goes:
time: 689 us; the launch traced here: 688 us
  waiting for transfers between devices  529 us (77%)
  matrix products  38.3 us (6%)
  starting transfers between devices  32.2 us (5%)
  blocking collectives  29.2 us (4%)
  local copies, waits for them, and re-layouts  21.9 us (3%)
  other arithmetic  21.5 us (3%)
  between operations  16.3 us (2%)
    reduce_scatter x1, waiting for transfers between devices, shards(): lax.psum_scatter(partial_gate.astype(jnp.bfloat16), 'dp', scatter_dimensi...  124 us
    reduce_scatter x1, waiting for transfers between devices, shards(): lax.psum_scatter(partial_up.astype(jnp.bfloat16), 'dp', scatter_dimension...  124 us
    all_gather x1, waiting for transfers between devices, shards(): lax.all_gather(mate_shares[0], 'dp', axis=0, tiled=True)  79.6 us
    all_gather x1, waiting for transfers between devices, shards(): lax.all_gather(mate_shares[2], 'dp', axis=1, tiled=True)  79 us
    reduce_scatter x1, waiting for transfers between devices, shards(): lax.psum_scatter(partial_down.astype(jnp.bfloat16), 'dp', scatter_dimensi...  45 us
    all_gather x1, waiting for transfers between devices, shards(): lax.all_gather(mate_shares[1], 'dp', axis=0, tiled=True)  34.6 us
    all_to_all x2, blocking collectives, shards(): lax.all_to_all(as_sent(outgoing), 'expert', split_axis=0, concat_axis=0,...  29.2 us
    all_to_all x1, waiting for transfers between devices, shards(): lax.all_to_all(expert_out.reshape(groups, capacity, model_width), 'expert...  15.8 us
  transfers between devices with their start and end apart: 11, of which 10 were waited for; matrix products, arithmetic and copies ran while one was open for 10% of the time, Pallas kernels for 0%

commit v1 on v0

--- a/solution.py
+++ b/solution.py
@@ -71,7 +71,9 @@
     gate_mat, up_mat, down_mat = (
         lax.all_gather(mate_shares[0], "dp", axis=0, tiled=True),
         lax.all_gather(mate_shares[1], "dp", axis=0, tiled=True),
-        lax.all_gather(mate_shares[2], "dp", axis=1, tiled=True),
+        jnp.concatenate(
+            lax.all_to_all(jnp.stack([mate_shares[2]] * lax.axis_size("dp")), "dp", 0, 0), axis=1
+        ),
     )
     repeated = jnp.repeat(tokens, top_count, axis=0)
     outgoing_rows = jnp.dot(place_mat, repeated, preferred_element_type=jnp.float32).astype(

time: 689 us -> 625 us (0.907)
  waiting for transfers between devices: 529 us -> 467 us
  blocking collectives: 29.2 us -> 0 us
  starting transfers between devices: 32.2 us -> 55 us
    all_gather x1 -> x0, waiting for transfers between devices: 79 us -> none  [shards(): lax.all_gather(mate_shares[2], 'dp', axis=1, tiled=True)]
    all_to_all x0 -> x1, waiting for transfers between devices: none -> 75.4 us  [shards(): lax.all_to_all(jnp.stack([mate_shares[2]] * lax.axis_size('dp')), 'dp', 0...]
    all_gather x1, waiting for transfers between devices: 79.6 us -> 21.5 us  [shards(): lax.all_gather(mate_shares[0], 'dp', axis=0, tiled=True)]
    all_gather x1, waiting for transfers between devices: 34.6 us -> 0.01 us  [shards(): lax.all_gather(mate_shares[1], 'dp', axis=0, tiled=True)]
    all_to_all x2 -> x0, blocking collectives: 29.2 us -> none  [shards(): lax.all_to_all(as_sent(outgoing), 'expert', split_axis=0, concat_axis=0,...]
    all_to_all x1, waiting for transfers between devices: 0.01 us -> 14.6 us  [shards(): lax.all_to_all(outgoing_grads.reshape(groups, capacity, model_width), 'ex...]
    all_to_all x0 -> x1, starting transfers between devices: none -> 13 us  [shards(): lax.all_to_all(jnp.stack([mate_shares[2]] * lax.axis_size('dp')), 'dp', 0...]
    all_to_all x1 -> x3, starting transfers between devices: 6.32 us -> 18.2 us  [shards(): lax.all_to_all(as_sent(outgoing), 'expert', split_axis=0, concat_axis=0,...]
  transfers between devices with their start and end apart: 11 -> 13, of which waited for: 10 -> 12; matrix products, arithmetic and copies ran while one was open for 10% -> 11% of each run, Pallas kernels for 0% -> 0%
where the time goes in v1:
time: 625 us; the launch traced here: 624 us
  waiting for transfers between devices  467 us (75%)
  starting transfers between devices  55 us (9%)
  matrix products  37 us (6%)
  local copies, waits for them, and re-layouts  27.2 us (4%)
  other arithmetic  22 us (4%)
  between operations  15.9 us (3%)
    reduce_scatter x1, waiting for transfers between devices, shards(): lax.psum_scatter(partial_up.astype(jnp.bfloat16), 'dp', scatter_dimension...  124 us
    reduce_scatter x1, waiting for transfers between devices, shards(): lax.psum_scatter(partial_gate.astype(jnp.bfloat16), 'dp', scatter_dimensi...  124 us
    all_to_all x1, waiting for transfers between devices, shards(): lax.all_to_all(jnp.stack([mate_shares[2]] * lax.axis_size('dp')), 'dp', 0...  75.4 us
    reduce_scatter x1, waiting for transfers between devices, shards(): lax.psum_scatter(partial_down.astype(jnp.bfloat16), 'dp', scatter_dimensi...  47 us
    all_gather x1, waiting for transfers between devices, shards(): lax.all_gather(mate_shares[0], 'dp', axis=0, tiled=True)  21.5 us
    all_to_all x3, starting transfers between devices, shards(): lax.all_to_all(as_sent(outgoing), 'expert', split_axis=0, concat_axis=0,...  18.2 us
    all_to_all x3, waiting for transfers between devices, shards(): lax.all_to_all(as_sent(outgoing), 'expert', split_axis=0, concat_axis=0,...  17.5 us
    all_to_all x1, waiting for transfers between devices, shards(): lax.all_to_all(outgoing_rows.reshape(groups, capacity, model_width), 'exp...  16.4 us
  transfers between devices with their start and end apart: 13, of which 12 were waited for; matrix products, arithmetic and copies ran while one was open for 11% of the time, Pallas kernels for 0%

profile of v1, /device:TPU:4, one launch (start us, length us, event | category | flops | bytes accessed | tf_op | source)
XLA Modules:
  0.0 624.1 jit_solution(12209930963555576033)
XLA Ops:
  10.5 6.3 %all-to-all-start.2 = ((bf16[8,64,768]{2,1,0:T(8,128)(2,1)}), bf16[8,64,768]{2,1,0:T(8,128)(2,1)}, u32[]{:S(2)}, u32[]{:S(2)}) async-start(bf16[8,64,768]{2,1,0:T(8,128)(2,1)} %get-tuple-element.27), calls=%async_computation.2 | async-start | bytes 1572864 | tf_op jit(solution)/shard_map/all_to_all | solution.py:67
  19.3 7.3 %all-to-all-done.2 = bf16[8,64,768]{2,1,0:T(8,128)(2,1)} async-done(((bf16[8,64,768]{2,1,0:T(8,128)(2,1)}), bf16[8,64,768]{2,1,0:T(8,128)(2,1)}, u32[]{:S(2)}, u32[]{:S(2)}) %all-to-all-start.2) | async-done | bytes 786464 | tf_op jit(solution)/shard_map/all_to_all | solution.py:67
  29.5 5.6 all-to-all-start.3
  36.0 8.6 %all-to-all-done.3 = bf16[8,768,64]{1,2,0:T(8,128)(2,1)S(1)} async-done(((bf16[8,768,64]{1,2,0:T(8,128)(2,1)}), bf16[8,768,64]{1,2,0:T(8,128)(2,1)S(1)}, u32[]{:S(2)}, u32[]{:S(2)}) %all-to-all-start.3) | async-done | bytes 786464 | tf_op jit(solution)/shard_map/all_to_all | solution.py:67
  44.7 6.3 %all-to-all-start.1 = ((bf16[8,64,768]{2,1,0:T(8,128)(2,1)}), bf16[8,64,768]{2,1,0:T(8,128)(2,1)}, u32[]{:S(2)}, u32[]{:S(2)}) async-start(bf16[8,64,768]{2,1,0:T(8,128)(2,1)} %get-tuple-element.26), calls=%async_computation.1 | async-start | bytes 1572864 | tf_op jit(solution)/shard_map/all_to_all | solution.py:67
  53.7 2.7 mul.84
  60.0 6.3 %all-to-all-start.6 = ((bf16[8,40,2048]{2,1,0:T(8,128)(2,1)}), bf16[8,40,2048]{2,1,0:T(8,128)(2,1)}, u32[]{:S(2)}, u32[]{:S(2)}) async-start(bf16[8,40,2048]{2,1,0:T(8,128)(2,1)} %bitcast.70), calls=%async_computation.6 | async-start | bytes 2621440 | tf_op jit(solution)/shard_map/all_to_all | solution.py:117
  66.3 14.6 %all-to-all-done.6 = bf16[8,40,2048]{2,1,0:T(8,128)(2,1)} async-done(((bf16[8,40,2048]{2,1,0:T(8,128)(2,1)}), bf16[8,40,2048]{2,1,0:T(8,128)(2,1)}, u32[]{:S(2)}, u32[]{:S(2)}) %all-to-all-start.6) | async-done | bytes 1310752 | tf_op jit(solution)/shard_map/all_to_all | solution.py:117
  83.0 13.0 %all-to-all-start.4 = ((bf16[32,768,64]{1,2,0:T(8,128)(2,1)}), bf16[32,768,64]{1,2,0:T(8,128)(2,1)}, u32[]{:S(2)}, u32[]{:S(2)}) async-start(bf16[32,768,64]{1,2,0:T(8,128)(2,1)} %stack.2), calls=%async_computation.4 | async-start | bytes 6291456 | tf_op jit(solution)/shard_map/all_to_all | solution.py:75
  100.4 75.4 %all-to-all-done.4 = bf16[32,768,64]{1,2,0:T(8,128)(2,1)} async-done(((bf16[32,768,64]{1,2,0:T(8,128)(2,1)}), bf16[32,768,64]{1,2,0:T(8,128)(2,1)}, u32[]{:S(2)}, u32[]{:S(2)}) %all-to-all-start.4) | async-done | bytes 3145760 | tf_op jit(solution)/shard_map/all_to_all | solution.py:75
  175.8 4.9 all-to-all-start
  180.7 3.5 fusion.20
  184.2 16.4 %all-to-all-done = bf16[8,40,2048]{2,1,0:T(8,128)(2,1)S(1)} async-done(((bf16[8,40,2048]{2,1,0:T(8,128)(2,1)}), bf16[8,40,2048]{2,1,0:T(8,128)(2,1)S(1)}, u32[]{:S(2)}, u32[]{:S(2)}) %all-to-all-start) | async-done | bytes 1310752 | tf_op jit(solution)/shard_map/all_to_all | solution.py:82
  200.6 4.0 fusion.2
  204.6 21.5 %all-gather.5.cloned.1.call-done = bf16[1,2048,768]{2,1,0:T(8,128)(2,1)} async-done(((bf16[1,64,768]{2,1,0:T(8,128)(2,1)}), bf16[1,2048,768]{2,1,0:T(8,128)(2,1)}) %all-gather.5.cloned.1.call-update) | async-done | bytes 3145744 | tf_op jit(solution)/shard_map/all_gather | solution.py:72
  226.1 4.4 multiply_convert_fusion.3
  231.3 4.8 convolution_convert_fusion
  236.4 3.5 convolution_convert_fusion.1
  240.9 3.5 convolution_convert_fusion.2
  245.5 4.3 convolution_convert_fusion.4
  249.8 5.0 all-to-all-start.5
  254.7 3.3 fusion
  260.4 11.3 %all-to-all-done.5 = bf16[8,40,2048]{2,1,0:T(8,128)(2,1)S(1)} async-done(((bf16[8,40,2048]{2,1,0:T(8,128)(2,1)}), bf16[8,40,2048]{2,1,0:T(8,128)(2,1)S(1)}, u32[]{:S(2)}, u32[]{:S(2)}) %all-to-all-start.5) | async-done | bytes 1310752 | tf_op jit(solution)/shard_map/all_to_all | solution.py:94
  271.7 7.2 %all-to-all-start.7 = ((bf16[8,40,2048]{2,1,0:T(8,128)(2,1)}), bf16[8,40,2048]{2,1,0:T(8,128)(2,1)S(1)}, u32[]{:S(2)}, u32[]{:S(2)}) async-start(bf16[8,40,2048]{2,1,0:T(8,128)(2,1)} %bitcast.75), calls=%async_computation.7 | async-start | bytes 2621440 | tf_op jit(solution)/shard_map/all_to_all | solution.py:132
  281.3 14.7 %all-to-all-done.7 = bf16[8,40,2048]{2,1,0:T(8,128)(2,1)S(1)} async-done(((bf16[8,40,2048]{2,1,0:T(8,128)(2,1)}), bf16[8,40,2048]{2,1,0:T(8,128)(2,1)S(1)}, u32[]{:S(2)}, u32[]{:S(2)}) %all-to-all-start.7) | async-done | bytes 1310752 | tf_op jit(solution)/shard_map/all_to_all | solution.py:132
  298.3 2.5 broadcast_select_fusion
  303.0 2.7 reshape.111
  306.9 4.7 reduce.1
  311.7 5.6 multiply_reduce_fusion.1
  317.3 47.0 %reduce-scatter.8.cloned.1.call-done = bf16[768,64]{0,1:T(8,128)(2,1)} async-done(((bf16[768,2048]{0,1:T(8,128)(2,1)}), bf16[768,64]{0,1:T(8,128)(2,1)}) %reduce-scatter.8.cloned.1.call-update) | async-done | bytes 98320 | tf_op jit(solution)/shard_map/reduce_scatter | solution.py:155
  365.9 124.3 %reduce-scatter.6.cloned.1.call-done = bf16[64,768]{1,0:T(8,128)(2,1)} async-done(((bf16[2048,768]{1,0:T(8,128)(2,1)}), bf16[64,768]{1,0:T(8,128)(2,1)}) %reduce-scatter.6.cloned.1.call-update) | async-done | bytes 98320 | tf_op jit(solution)/shard_map/reduce_scatter | solution.py:152
  491.8 124.2 %reduce-scatter.4.cloned.1.call-done = bf16[64,768]{1,0:T(8,128)(2,1)} async-done(((bf16[2048,768]{1,0:T(8,128)(2,1)}), bf16[64,768]{1,0:T(8,128)(2,1)}) %reduce-scatter.4.cloned.1.call-update) | async-done | bytes 98320 | tf_op jit(solution)/shard_map/reduce_scatter | solution.py:149
  (82 shorter events, 38.6 us)
Async XLA Ops:
  7.2 21.0 %copy-start = (bf16[1,768,2048]{2,1,0:T(8,128)(2,1)S(1)}, bf16[1,768,2048]{2,1,0:T(8,128)(2,1)}, u32[]{:S(2)}) copy-start(bf16[1,768,2048]{2,1,0:T(8,128)(2,1)} %param.17) | copy-start | bytes 9437188
  7.2 9.6 %copy-start.10 = (s32[8]{0:T(128)S(1)}, s32[8]{0:T(128)}, u32[]{:S(2)}) copy-start(s32[8]{0:T(128)} %param.14) | copy-start | bytes 100
  10.5 16.1 %all-to-all-start.2 = ((bf16[8,64,768]{2,1,0:T(8,128)(2,1)}), bf16[8,64,768]{2,1,0:T(8,128)(2,1)}, u32[]{:S(2)}, u32[]{:S(2)}) async-start(bf16[8,64,768]{2,1,0:T(8,128)(2,1)} %get-tuple-element.27), calls=%async_computation.2 | async-start | bytes 1572864 | tf_op jit(solution)/shard_map/all_to_all | solution.py:67
  16.8 18.3 %copy-start.8 = (s32[128,2]{0,1:T(2,128)S(1)}, s32[128,2]{0,1:T(2,128)}, u32[]{:S(2)}) copy-start(s32[128,2]{0,1:T(2,128)} %param.12) | copy-start | bytes 3076
  16.8 183.8 %all-gather.7.cloned.1.call-start = ((), (), s32[]{:S(2)}) async-start(), calls=%async_computation.15 | async-start | bytes 3244032 | tf_op jit(solution)/shard_map/all_gather | solution.py:73
  28.5 22.8 %copy-start.6 = (bf16[128,2048]{1,0:T(8,128)(2,1)S(1)}, bf16[128,2048]{1,0:T(8,128)(2,1)}, u32[]{:S(2)}) copy-start(bf16[128,2048]{1,0:T(8,128)(2,1)} %param.11) | copy-start | bytes 1572868
  29.5 15.2 %all-to-all-start.3 = ((bf16[8,768,64]{1,2,0:T(8,128)(2,1)}), bf16[8,768,64]{1,2,0:T(8,128)(2,1)S(1)}, u32[]{:S(2)}, u32[]{:S(2)}) async-start(bf16[8,768,64]{1,2,0:T(8,128)(2,1)} %broadcast_select_fusion.1), calls=%async_computation.3 | async-start | bytes 1572864 | tf_op jit(solution)/shard_map/all_to_all | solution.py:67
  44.7 15.3 %all-to-all-start.1 = ((bf16[8,64,768]{2,1,0:T(8,128)(2,1)}), bf16[8,64,768]{2,1,0:T(8,128)(2,1)}, u32[]{:S(2)}, u32[]{:S(2)}) async-start(bf16[8,64,768]{2,1,0:T(8,128)(2,1)} %get-tuple-element.26), calls=%async_computation.1 | async-start | bytes 1572864 | tf_op jit(solution)/shard_map/all_to_all | solution.py:67
  53.7 2.7 copy-start.9
  56.4 3.6 copy-start.2
  60.0 20.9 %all-to-all-start.6 = ((bf16[8,40,2048]{2,1,0:T(8,128)(2,1)}), bf16[8,40,2048]{2,1,0:T(8,128)(2,1)}, u32[]{:S(2)}, u32[]{:S(2)}) async-start(bf16[8,40,2048]{2,1,0:T(8,128)(2,1)} %bitcast.70), calls=%async_computation.6 | async-start | bytes 2621440 | tf_op jit(solution)/shard_map/all_to_all | solution.py:117
  83.0 14.6 %copy-start.7 = (bf16[128,2048]{1,0:T(8,128)(2,1)S(1)}, bf16[128,2048]{1,0:T(8,128)(2,1)}, u32[]{:S(2)}) copy-start(bf16[128,2048]{1,0:T(8,128)(2,1)} %param.10) | copy-start | bytes 1572868
  83.0 92.8 %all-to-all-start.4 = ((bf16[32,768,64]{1,2,0:T(8,128)(2,1)}), bf16[32,768,64]{1,2,0:T(8,128)(2,1)}, u32[]{:S(2)}, u32[]{:S(2)}) async-start(bf16[32,768,64]{1,2,0:T(8,128)(2,1)} %stack.2), calls=%async_computation.4 | async-start | bytes 6291456 | tf_op jit(solution)/shard_map/all_to_all | solution.py:75
  96.0 130.1 %all-gather.5.cloned.1.call-start = ((), (), s32[]{:S(2)}) async-start(), calls=%async_computation.14 | async-start | bytes 3244032 | tf_op jit(solution)/shard_map/all_gather | solution.py:72
  175.8 24.8 %all-to-all-start = ((bf16[8,40,2048]{2,1,0:T(8,128)(2,1)}), bf16[8,40,2048]{2,1,0:T(8,128)(2,1)S(1)}, u32[]{:S(2)}, u32[]{:S(2)}) async-start(bf16[8,40,2048]{2,1,0:T(8,128)(2,1)} %bitcast.3), calls=%async_computation | async-start | bytes 2621440 | tf_op jit(solution)/shard_map/all_to_all | solution.py:82
  180.7 183.6 %reduce-scatter.8.cloned.1.call-start = ((), (), s32[]{:S(2)}) async-start(), calls=%async_computation.13 | async-start | bytes 3244032 | tf_op jit(solution)/shard_map/reduce_scatter | solution.py:155
  230.5 0.8 copy-start.13
  236.1 254.1 %reduce-scatter.6.cloned.1.call-start = ((), (), s32[]{:S(2)}) async-start(), calls=%async_computation.12 | async-start | bytes 3244032 | tf_op jit(solution)/shard_map/reduce_scatter | solution.py:152
  239.8 1.0 copy-start.12
  239.9 376.1 %reduce-scatter.4.cloned.1.call-start = ((), (), s32[]{:S(2)}) async-start(), calls=%async_computation.11 | async-start | bytes 3244032 | tf_op jit(solution)/shard_map/reduce_scatter | solution.py:149
  244.4 1.1 copy-start.14
  249.8 21.9 %all-to-all-start.5 = ((bf16[8,40,2048]{2,1,0:T(8,128)(2,1)}), bf16[8,40,2048]{2,1,0:T(8,128)(2,1)S(1)}, u32[]{:S(2)}, u32[]{:S(2)}) async-start(bf16[8,40,2048]{2,1,0:T(8,128)(2,1)} %bitcast.14), calls=%async_computation.5 | async-start | bytes 2621440 | tf_op jit(solution)/shard_map/all_to_all | solution.py:94
  254.7 3.3 copy-start.11
  271.7 24.3 %all-to-all-start.7 = ((bf16[8,40,2048]{2,1,0:T(8,128)(2,1)}), bf16[8,40,2048]{2,1,0:T(8,128)(2,1)S(1)}, u32[]{:S(2)}, u32[]{:S(2)}) async-start(bf16[8,40,2048]{2,1,0:T(8,128)(2,1)} %bitcast.75), calls=%async_computation.7 | async-start | bytes 2621440 | tf_op jit(solution)/shard_map/all_to_all | solution.py:132
  296.0 2.3 copy-start.4
  300.8 4.9 copy-start.5
  303.0 2.7 copy-start.3
  306.9 310.6 %copy-start.1 = (bf16[1,768,2048]{2,1,0:T(8,128)(2,1)S(1)}, bf16[1,768,2048]{2,1,0:T(8,128)(2,1)}, u32[]{:S(2)}) copy-start(bf16[1,768,2048]{2,1,0:T(8,128)(2,1)} %param.17) | copy-start | bytes 9437188
Sparse Core Ops, SparseCore 0:
  28.3 94.7 all-gather.6
  126.5 99.5 all-gather.4
  236.2 128.0 reduce-scatter.7
  368.3 121.7 reduce-scatter.5
  494.2 121.7 reduce-scatter.3
